TPU v7x, 32 devices: a whole 2x2x4 slice. The times are simulated.
32 devices in a mesh: clip: 2 (over x), trow: 8 (over z, y), tcol: 2 (over core).
Axes of the slice: x: 2, y: 2, z: 4, core: 2. Of those that a mesh axis runs over, the one named last changes fastest.
Arguments:
- field: bfloat16 [8, 2048, 8192], P(None, ('clip', 'trow'), 'tcol'), parts along dimension 1, may hold values from -6 to 6
- pointwise: bfloat16 [2, 8, 8], replicated, may hold values from -2 to 2
- mixing: bfloat16 [2, 2, 8, 8, 4608], replicated, may hold values from -2 to 2
- project: bfloat16 [8], replicated, may hold values from -2 to 2
Outputs:
- image: bfloat16 [2048, 8192], P(('clip', 'trow'), 'tcol'), parts along dimension 0
There are 2 independent parts, one for each index of `clip`. A program takes and returns all parts, laid end to end along the dimension named above; an argument that names none is the same for every part. Nothing has to cross between parts.
All inputs are finite; a program needn't handle non-finite values.
Results may differ from a plain program's by a relative error of at most 0.0084.
Values sent between devices are 32-bit elements; how exact they have to be, the bound alone decides.
A program may use at most 128 MiB of HBM per device.

v0:
```python
import functools
import math

import jax
import jax.numpy as jnp
from jax import lax
from jax.experimental import pallas as pl
from jax.experimental.pallas import tpu as pltpu
from jax.sharding import PartitionSpec as P

KY = 48
LAYERS = 2
LANES = 128
SUB = 8
XB = 16
MESH = pl.DeviceIdType.MESH
VMEM_BYTES = 60 * 1024 * 1024


def tile_of(cols):
    for size in (512, 256, 128):
        if cols % size == 0:
            return size
    return cols


def column_rows(start, count, total):
    columns = start + jnp.arange(count, dtype=jnp.int32)
    freqs = jnp.arange(KY, dtype=jnp.int32)
    phase = freqs[:, None] * columns[None, :] % total
    angle = phase.astype(jnp.float32) * (2.0 * math.pi / total)
    cosine = jnp.cos(angle).astype(jnp.bfloat16)
    sine = (-jnp.sin(angle)).astype(jnp.bfloat16)
    blank = jnp.zeros((LANES - 2 * KY, count), jnp.bfloat16)
    return jnp.concatenate([cosine, sine, blank, sine, -cosine, blank], axis=0)


def row_tables(start, count, total, owners, per, rows):
    owner = jnp.arange(owners * rows, dtype=jnp.int32) // rows
    local = jnp.arange(owners * rows, dtype=jnp.int32) % rows
    index = owner * per + local
    valid = (local < per) & (index < 2 * KY)
    freqs = jnp.where(index < KY, index, index + (total - 2 * KY))
    freqs = jnp.where(valid, freqs, 0)
    places = start + jnp.arange(count, dtype=jnp.int32)
    phase = freqs[:, None] * places[None, :] % total
    angle = phase.astype(jnp.float32) * (2.0 * math.pi / total)
    keep = valid[:, None]
    return jnp.where(keep, jnp.cos(angle), 0.0), jnp.where(keep, jnp.sin(angle), 0.0)


def transform_rows(channels, rows_here, scale, table_ref, acc, out_ref):
    for c in range(channels):
        here = pl.ds(c * rows_here, rows_here)
        pair = jnp.concatenate([acc[here, :LANES], acc[here, LANES:]], axis=0)
        part = jnp.dot(
            table_ref[...], pair, precision=lax.Precision.HIGHEST, preferred_element_type=jnp.float32
        )
        owners = out_ref.shape[0] * out_ref.shape[1]
        part = part * scale
        out_ref[:, :, c] = part.reshape(out_ref.shape[0], out_ref.shape[1], part.shape[0] // owners, LANES)


def accumulate(value, et_ref, acc):
    acc[...] += lax.dot_general(
        value, et_ref[...], (((1,), (1,)), ((), ())), preferred_element_type=jnp.float32
    )


def forward_kernel(scale, field_ref, et_ref, table_ref, out_ref, acc):
    channels, rows_here, cols = field_ref.shape
    step = pl.program_id(0)

    @pl.when(step == 0)
    def _():
        acc[...] = jnp.zeros_like(acc)

    accumulate(field_ref[...].reshape(channels * rows_here, cols), et_ref, acc)

    @pl.when(step == pl.num_programs(0) - 1)
    def _():
        transform_rows(channels, rows_here, scale, table_ref, acc, out_ref)


def prepare_hidden(y_ref, inverse_ref, hidden):
    channels = y_ref.shape[2]
    rows_here = inverse_ref.shape[0]
    depth = inverse_ref.shape[1] // 2
    lane = lax.broadcasted_iota(jnp.int32, (depth, LANES), 1)
    for o in range(channels):
        here = y_ref[:, :, o].reshape(depth, LANES)
        turned = jnp.where(lane < KY, -pltpu.roll(here, LANES - KY, 1), pltpu.roll(here, KY, 1))
        turned = jnp.where(lane < 2 * KY, turned, 0.0)
        part = jnp.dot(
            inverse_ref[...],
            jnp.concatenate([here, turned], axis=0),
            precision=lax.Precision.HIGHEST,
            preferred_element_type=jnp.float32,
        ).astype(jnp.bfloat16)
        for block in range(rows_here // XB):
            start = (block * channels + o) * XB
            hidden[start : start + XB, :] = part[block * XB : (block + 1) * XB]


def spectral_values(et_ref, hidden, spectral):
    spectral[...] = jnp.dot(hidden[...], et_ref[:LANES, :], preferred_element_type=jnp.float32)


def block_update(block, value_ref, kron_ref, spectral):
    channels, _, cols = value_ref.shape
    size = channels * XB
    value = value_ref[:, block * XB : (block + 1) * XB, :].reshape(size, cols)
    local = jnp.dot(kron_ref[...], value, preferred_element_type=jnp.float32)
    return jnp.tanh(local + spectral[block * size : (block + 1) * size, :] * (1.0 / KY))


def middle_kernel(scale, value_ref, et_ref, y_ref, inverse_ref, kron_ref, table_ref, next_ref, out_ref, hidden, spectral, acc):
    channels, rows_here, cols = value_ref.shape
    step = pl.program_id(0)

    @pl.when(step == 0)
    def _():
        acc[...] = jnp.zeros_like(acc)
        prepare_hidden(y_ref, inverse_ref, hidden)

    spectral_values(et_ref, hidden, spectral)
    for block in range(rows_here // XB):
        updated = block_update(block, value_ref, kron_ref, spectral).astype(jnp.bfloat16)
        next_ref[:, block * XB : (block + 1) * XB, :] = updated.reshape(channels, XB, cols)
    accumulate(next_ref[...].reshape(channels * rows_here, cols), et_ref, acc)

    @pl.when(step == pl.num_programs(0) - 1)
    def _():
        transform_rows(channels, rows_here, scale, table_ref, acc, out_ref)


def last_kernel(value_ref, et_ref, y_ref, inverse_ref, kron_ref, project_ref, image_ref, hidden, spectral):
    channels, rows_here, cols = value_ref.shape

    @pl.when(pl.program_id(0) == 0)
    def _():
        prepare_hidden(y_ref, inverse_ref, hidden)

    spectral_values(et_ref, hidden, spectral)
    for block in range(rows_here // XB):
        updated = block_update(block, value_ref, kron_ref, spectral).reshape(channels, XB, cols)
        total = project_ref[0] * updated[0]
        for c in range(1, channels):
            total = total + project_ref[c] * updated[c]
        image_ref[block * XB : (block + 1) * XB, :] = total.astype(jnp.bfloat16)


def exchange_kernel(
    groups, spectrum_ref, same_ref, cross_ref, out_ref, partner_part, mine, arrived, mixed,
    pair_send, pair_recv, sum_send, sum_recv, mix_send, mix_recv, relay_send, relay_recv,
):
    clip = lax.axis_index("clip")
    row = lax.axis_index("trow")
    core = lax.axis_index("tcol")
    other = 1 - core
    channels = spectrum_ref.shape[2]

    barrier = pltpu.get_barrier_semaphore()
    pl.semaphore_signal(barrier, inc=1, device_id=(clip, row, other), device_id_type=MESH)
    for j in range(1, groups):
        peer = lax.rem(row + j, groups)
        pl.semaphore_signal(barrier, inc=1, device_id=(clip, peer, core), device_id_type=MESH)
    pl.semaphore_wait(barrier, groups)

    pair = pltpu.make_async_remote_copy(
        src_ref=spectrum_ref.at[other],
        dst_ref=partner_part,
        send_sem=pair_send,
        recv_sem=pair_recv,
        device_id=(clip, row, other),
        device_id_type=MESH,
    )
    pair.start()
    pair.wait()

    mine[...] = spectrum_ref[core] + partner_part[...]
    sums = []
    for j in range(1, groups):
        peer = lax.rem(row + j, groups)
        copy = pltpu.make_async_remote_copy(
            src_ref=mine.at[peer],
            dst_ref=arrived.at[j - 1],
            send_sem=sum_send.at[j - 1],
            recv_sem=sum_recv.at[j - 1],
            device_id=(clip, peer, core),
            device_id_type=MESH,
        )
        copy.start()
        sums.append(copy)
    total = mine[row]
    for j in range(1, groups):
        sums[j - 1].wait_recv()
        total = total + arrived[j - 1]

    lane = lax.broadcasted_iota(jnp.int32, total.shape[1:], 1)
    plain = [total[c] for c in range(channels)]
    swapped = [
        jnp.where(lane < KY, pltpu.roll(s, LANES - KY, 1), pltpu.roll(s, KY, 1)) for s in plain
    ]
    for o in range(channels):
        value = same_ref[o, 0] * plain[0] + cross_ref[o, 0] * swapped[0]
        for c in range(1, channels):
            value = value + (same_ref[o, c] * plain[c] + cross_ref[o, c] * swapped[c])
        mixed[o] = value
    out_ref[core, row] = mixed[...]

    sends = []
    for j in range(1, groups):
        peer = lax.rem(row + j, groups)
        copy = pltpu.make_async_remote_copy(
            src_ref=mixed,
            dst_ref=out_ref.at[core, row],
            send_sem=mix_send.at[j - 1],
            recv_sem=mix_recv.at[j - 1],
            device_id=(clip, peer, core),
            device_id_type=MESH,
        )
        copy.start()
        sends.append(copy)
    relays = []
    for j in range(groups):
        source = lax.rem(row + groups - j, groups)
        if j:
            sends[j - 1].wait_recv()
        relay = pltpu.make_async_remote_copy(
            src_ref=mixed if j == 0 else out_ref.at[core, source],
            dst_ref=out_ref.at[core, source],
            send_sem=relay_send.at[j],
            recv_sem=relay_recv.at[j],
            device_id=(clip, row, other),
            device_id_type=MESH,
        )
        relay.start()
        relays.append(relay)
    for copy in sums + sends:
        copy.wait_send()
    for relay in relays:
        relay.wait()


def whole(shape):
    return pl.BlockSpec(shape, lambda i: (0,) * len(shape))


def exchange(spectrum, same, cross, groups, cid):
    chunk = spectrum.shape[2:]
    dma = pltpu.SemaphoreType.DMA
    vmem = pl.BlockSpec(memory_space=pltpu.VMEM)
    links = max(groups - 1, 1)
    return pl.pallas_call(
        functools.partial(exchange_kernel, groups),
        out_shape=jax.ShapeDtypeStruct(spectrum.shape, jnp.float32),
        in_specs=[vmem, vmem, vmem],
        out_specs=vmem,
        scratch_shapes=[
            pltpu.VMEM((groups,) + chunk, jnp.float32),
            pltpu.VMEM((groups,) + chunk, jnp.float32),
            pltpu.VMEM((links,) + chunk, jnp.float32),
            pltpu.VMEM(chunk, jnp.float32),
            dma(()), dma(()), dma((links,)), dma((links,)), dma((links,)), dma((links,)),
            dma((groups,)), dma((groups,)),
        ],
        compiler_params=pltpu.CompilerParams(
            collective_id=cid, has_side_effects=True, vmem_limit_bytes=VMEM_BYTES
        ),
        name=f"exchange_{cid}",
    )(spectrum, same, cross)


def body(groups, cores, field, pointwise, mixing, project):
    channels, rows_here, cols_here = field.shape
    total_rows = rows_here * groups
    total_cols = cols_here * cores
    row_index = lax.axis_index("trow")
    core_index = lax.axis_index("tcol")
    owners = groups * cores
    per = min(p for p in range(1, 2 * KY + 1) if 2 * KY % p == 0 and p * owners >= 2 * KY)
    sub = -(-per // SUB) * SUB
    scale = 1.0 / math.sqrt(total_rows * total_cols)
    tile = tile_of(cols_here)
    steps = cols_here // tile

    columns = column_rows(core_index * cols_here, cols_here, total_cols)
    cosine, sine = row_tables(row_index * rows_here, rows_here, total_rows, owners, per, sub)
    forward_table = jnp.concatenate([cosine, sine], axis=1)
    inverse_table = jnp.concatenate([cosine.T, sine.T], axis=1)

    first = (core_index * groups + row_index) * (per * KY)
    chunk = lax.dynamic_slice_in_dim(mixing, first, per * KY, 4)
    chunk = chunk.reshape(LAYERS, 2, channels, channels, per, KY).astype(jnp.float32)
    widths = ((0, 0), (0, 0), (0, 0), (0, sub - per), (0, LANES - 2 * KY))
    same = jnp.pad(jnp.concatenate([chunk[:, 0], chunk[:, 0]], axis=-1), widths)
    cross = jnp.pad(jnp.concatenate([-chunk[:, 1], chunk[:, 1]], axis=-1), widths)
    eye = jnp.eye(XB, dtype=jnp.bfloat16)
    krons = [jnp.kron(pointwise[layer], eye) for layer in range(LAYERS)]

    spectrum_shape = (cores, groups, channels, sub, LANES)
    spectrum_type = jax.ShapeDtypeStruct(spectrum_shape, jnp.float32)
    value_spec = pl.BlockSpec((channels, rows_here, tile), lambda i: (0, 0, i))
    et_spec = pl.BlockSpec((2 * LANES, tile), lambda i: (0, i))
    hidden = pltpu.VMEM((channels * rows_here, LANES), jnp.bfloat16)
    spectral = pltpu.VMEM((channels * rows_here, tile), jnp.float32)
    acc = pltpu.VMEM((channels * rows_here, 2 * LANES), jnp.float32)
    params = pltpu.CompilerParams(dimension_semantics=("arbitrary",), vmem_limit_bytes=VMEM_BYTES)

    spectrum = pl.pallas_call(
        functools.partial(forward_kernel, scale),
        grid=(steps,),
        out_shape=spectrum_type,
        in_specs=[value_spec, et_spec, whole(forward_table.shape)],
        out_specs=whole(spectrum_shape),
        scratch_shapes=[acc],
        compiler_params=params,
        name="forward",
    )(field, columns, forward_table)

    current = field
    for layer in range(LAYERS):
        y = exchange(spectrum, same[layer], cross[layer], groups, layer)
        specs = [value_spec, et_spec, whole(spectrum_shape), whole(inverse_table.shape), whole(krons[layer].shape)]
        if layer + 1 < LAYERS:
            current, spectrum = pl.pallas_call(
                functools.partial(middle_kernel, scale),
                grid=(steps,),
                out_shape=(jax.ShapeDtypeStruct(field.shape, jnp.bfloat16), spectrum_type),
                in_specs=specs + [whole(forward_table.shape)],
                out_specs=(value_spec, whole(spectrum_shape)),
                scratch_shapes=[hidden, spectral, acc],
                compiler_params=params,
                name="middle",
            )(current, columns, y, inverse_table, krons[layer], forward_table)
        else:
            image = pl.pallas_call(
                last_kernel,
                grid=(steps,),
                out_shape=jax.ShapeDtypeStruct((rows_here, cols_here), jnp.bfloat16),
                in_specs=specs + [pl.BlockSpec(memory_space=pltpu.SMEM)],
                out_specs=pl.BlockSpec((rows_here, tile), lambda i: (0, i)),
                scratch_shapes=[hidden, spectral],
                compiler_params=params,
                name="last",
            )(current, columns, y, inverse_table, krons[layer], project.astype(jnp.float32))
    return image


def solution(mesh):
    groups, cores = mesh.shape["trow"], mesh.shape["tcol"]
    in_specs = (P(None, ("clip", "trow"), "tcol"), P(), P(), P())
    out_specs = P(("clip", "trow"), "tcol")
    return jax.shard_map(
        functools.partial(body, groups, cores), mesh=mesh, in_specs=in_specs, out_specs=out_specs, check_vma=False
    )
```

profile of v0, /device:TPU:0, one launch (start us, length us, event | category | flops | bytes accessed | tf_op | source)
XLA Modules:
  0.0 106.1 jit_solution(10004194453587475199)
XLA Ops:
  0.0 1.2 %convert_element_type.45.project_ref = f32[8]{0:T(128)} convert(bf16[8]{0:T(256)(128)(2,1)} %param.7) | non-fusion elementwise | flops 8 | bytes 48 | tf_op jit(solution)/shard_map/convert_element_type | solution.py:347
  1.3 0.7 slice_bitcast_fusion.6
  2.0 0.6 cosine_select_fusion
  2.6 0.7 pad_maximum_fusion
  3.3 1.1 %dynamic-slice_convert_fusion = f32[2,2,8,8,288]{4,3,2,1,0:T(8,128)S(1)} fusion(bf16[2,2,8,8,4608]{4,3,2,1,0:T(8,128)(2,1)} %param.6, s32[]{:T(128)S(6)} %select_n.105), kind=kLoop, calls=%fused_computation.25 | loop fusion | flops 73728 | bytes 442372 | tf_op jit(solution)/shard_map/convert_element_type | solution.py:295
  4.4 0.1 broadcast_multiply_fusion
  4.5 0.8 mul.154.kron_ref
  5.3 0.8 mul.150.kron_ref
  6.1 0.3 reshape.67
  6.4 0.1 fusion.19
  6.4 0.1 slice_bitcast_fusion
  6.5 0.4 select_maximum_fusion
  6.9 0.8 slice_bitcast_fusion.2
  7.7 0.8 slice_bitcast_fusion.3
  8.6 2.9 %fusion.6 = bf16[256,4096]{1,0:T(8,128)(2,1)S(1)} fusion(s32[4096]{0:T(1024)S(1)} %iota_add_fusion), kind=kLoop, calls=%fused_computation.18 | loop fusion | flops 2949119 | bytes 409600
  11.5 3.0 %fusion.7 = bf16[256,4096]{1,0:T(8,128)(2,1)S(1)} fusion(bf16[256,4096]{1,0:T(8,128)(2,1)S(1)} %fusion.6, s32[4096]{0:T(1024)S(1)} %iota_add_fusion), kind=kLoop, calls=%fused_computation.19 | loop fusion | flops 3145728 | bytes 409600
  14.5 3.0 %fusion.8 = bf16[256,4096]{1,0:T(8,128)(2,1)S(1)} fusion(bf16[256,4096]{1,0:T(8,128)(2,1)S(1)} %broadcast_dynamic-update-slice_fusion, s32[4096]{0:T(1024)S(1)} %iota_add_fusion), kind=kLoop, calls=%fused_computation.20 | loop fusion | flops 3145728 | bytes 409600
  17.4 2.9 %negate_dynamic-update-slice_fusion = bf16[256,4096]{1,0:T(8,128)(2,1)S(1)} fusion(bf16[256,4096]{1,0:T(8,128)(2,1)S(1)} %fusion.8, s32[4096]{0:T(1024)S(1)} %iota_add_fusion), kind=kLoop, calls=%fused_computation.17 | loop fusion | flops 3538944 | bytes 409600
  20.4 0.0 copy-start
  20.4 1.4 %copy-done = bf16[256,4096]{1,0:T(8,128)(2,1)} copy-done((bf16[256,4096]{1,0:T(8,128)(2,1)}, bf16[256,4096]{1,0:T(8,128)(2,1)S(1)}, u32[]{:S(2)}) %copy-start) | copy-done | bytes 2097176
  21.8 9.7 %forward.1.spectrum_ref = f32[2,8,8,8,128]{4,3,2,1,0:T(8,128)} custom-call(bf16[8,128,4096]{2,1,0:T(8,128)(2,1)} %value_ref.1, bf16[256,4096]{1,0:T(8,128)(2,1)} %copy-done, f32[128,256]{1,0:T(8,128)} %get-tuple-element.23.table_ref), custom_call_target="tpu_custom_call" | custom-call | tf_op jit(solution)/shard_map/forward/pallas_call | solution.py:311
  31.4 23.9 %exchange_0.1.y_ref = f32[2,8,8,8,128]{4,3,2,1,0:T(8,128)} custom-call(f32[2,8,8,8,128]{4,3,2,1,0:T(8,128)} %forward.1.spectrum_ref, f32[8,8,8,128]{3,2,1,0:T(8,128)} %get-tuple-element.14.same_ref, f32[8,8,8,128]{3,2,1,0:T(8,128)} %get-tuple-element.12.cross_ref), custom_call_target="tpu_custom_call" | custom-call | tf_op jit(solution)/shard_map/exchange_0/pallas_call | solution.py:255
  55.3 16.8 %middle.1 = (bf16[8,128,4096]{2,1,0:T(8,128)(2,1)}, f32[2,8,8,8,128]{4,3,2,1,0:T(8,128)}) custom-call(bf16[8,128,4096]{2,1,0:T(8,128)(2,1)} %value_ref.1, bf16[256,4096]{1,0:T(8,128)(2,1)} %copy-done, f32[2,8,8,8,128]{4,3,2,1,0:T(8,128)} %exchange_0.1.y_ref, f32[128,256]{1,0:T(8,128)} %get-tuple-element.24.inverse_ref, bf16[128,128]{1,0:T(8,128)(2,1)} %mul.150.kron_ref, ...), custom_call_target="tpu_custom_call" | custom-call | tf_op jit(solution)/shard_map/middle/pallas_call | solution.py:327
  72.1 22.4 %exchange_1.1.y_ref = f32[2,8,8,8,128]{4,3,2,1,0:T(8,128)} custom-call(f32[2,8,8,8,128]{4,3,2,1,0:T(8,128)} %get-tuple-element.8.spectrum_ref, f32[8,8,8,128]{3,2,1,0:T(8,128)} %get-tuple-element.13.same_ref, f32[8,8,8,128]{3,2,1,0:T(8,128)} %get-tuple-element.11.cross_ref), custom_call_target="tpu_custom_call" | custom-call | tf_op jit(solution)/shard_map/exchange_1/pallas_call | solution.py:255
  94.6 11.6 %last.1 = bf16[128,4096]{1,0:T(8,128)(2,1)} custom-call(bf16[8,128,4096]{2,1,0:T(8,128)(2,1)} %get-tuple-element.7.value_ref, bf16[256,4096]{1,0:T(8,128)(2,1)} %copy-done, f32[2,8,8,8,128]{4,3,2,1,0:T(8,128)} %exchange_1.1.y_ref, f32[128,256]{1,0:T(8,128)} %get-tuple-element.24.inverse_ref, bf16[128,128]{1,0:T(8,128)(2,1)} %mul.154.kron_ref, ...), custom_call_target="tpu_custom_call" | custom-call | tf_op jit(solution)/shard_map/last/pallas_call | solution.py:338
  (7 shorter events, 0.1 us)
Async XLA Ops:
  20.4 1.4 %copy-start = (bf16[256,4096]{1,0:T(8,128)(2,1)}, bf16[256,4096]{1,0:T(8,128)(2,1)S(1)}, u32[]{:S(2)}) copy-start(bf16[256,4096]{1,0:T(8,128)(2,1)S(1)} %broadcast_dynamic-update-slice_fusion.1.et_ref) | copy-start | bytes 6291460
where the time goes:
time: 107 us; the launch traced here: 106 us
  Pallas kernels  84.4 us (79%)
  other arithmetic  15.9 us (15%)
  local copies, waits for them, and re-layouts  5.71 us (5%)
    pallas_call x2, Pallas kernels, exchange(): pl.pallas_call(functools.partial(exchange_kernel, groups), out_shape=jax....  46.3 us
    pallas_call x1, Pallas kernels, body(): pl.pallas_call(functools.partial(middle_kernel, scale), grid=(steps,), ou...  16.8 us
    unnamed x4, other arithmetic  11.7 us
    pallas_call x1, Pallas kernels, body(): pl.pallas_call(last_kernel, grid=(steps,), out_shape=jax.ShapeDtypeStruct...  11.6 us
    pallas_call x1, Pallas kernels, body(): pl.pallas_call(functools.partial(forward_kernel, scale), grid=(steps,), o...  9.69 us
    mul x3, local copies, waits for them, and re-layouts, body(): krons = [jnp.kron(pointwise[layer], eye) for layer in range(LAYERS)]  2.27 us

commit v1 on v0

v1 whole, which is shorter than its diff:
```python
import functools
import math

import jax
import jax.numpy as jnp
from jax import lax
from jax.experimental import pallas as pl
from jax.experimental.pallas import tpu as pltpu
from jax.sharding import PartitionSpec as P

KY = 48
LAYERS = 2
LANES = 128
SUB = 8
XB = 16
MESH = pl.DeviceIdType.MESH
VMEM_BYTES = 60 * 1024 * 1024


def tile_of(cols):
    for size in (512, 256, 128):
        if cols % size == 0:
            return size
    return cols


def phase_angle(columns, total):
    freqs = jnp.arange(KY, dtype=jnp.int32)
    phase = freqs[:, None] * columns[None, :] % total
    return phase.astype(jnp.float32) * (2.0 * math.pi / total)


def column_seeds(start, count, tile, total):
    coarse = phase_angle(start + jnp.arange(count // LANES, dtype=jnp.int32) * LANES, total)
    coarse = coarse.reshape(KY, count // tile, tile // LANES).transpose(1, 0, 2)
    fine = phase_angle(jnp.arange(LANES, dtype=jnp.int32), total)
    return (
        jnp.concatenate([jnp.cos(coarse), jnp.sin(coarse)], axis=1),
        jnp.concatenate([jnp.cos(fine), jnp.sin(fine)], axis=0),
    )


def row_tables(start, count, total, owners, per, rows):
    owner = jnp.arange(owners * rows, dtype=jnp.int32) // rows
    local = jnp.arange(owners * rows, dtype=jnp.int32) % rows
    index = owner * per + local
    valid = (local < per) & (index < 2 * KY)
    freqs = jnp.where(index < KY, index, index + (total - 2 * KY))
    freqs = jnp.where(valid, freqs, 0)
    places = start + jnp.arange(count, dtype=jnp.int32)
    phase = freqs[:, None] * places[None, :] % total
    angle = phase.astype(jnp.float32) * (2.0 * math.pi / total)
    keep = valid[:, None]
    return jnp.where(keep, jnp.cos(angle), 0.0), jnp.where(keep, jnp.sin(angle), 0.0)


def transform_rows(channels, rows_here, scale, table_ref, acc, out_ref):
    cores, groups = out_ref.shape[:2]
    out_ref[...] = jnp.zeros_like(out_ref)
    for c in range(channels):
        sums = acc[:, c * rows_here : (c + 1) * rows_here]
        turned = jnp.concatenate([sums[KY:], -sums[:KY]], axis=0)
        part = lax.dot_general(
            table_ref[...],
            jnp.concatenate([sums, turned], axis=1),
            (((1,), (1,)), ((), ())),
            precision=lax.Precision.HIGHEST,
            preferred_element_type=jnp.float32,
        )
        part = part * scale
        out_ref[:, :, c, :, : 2 * KY] = part.reshape(cores, groups, part.shape[0] // (cores * groups), 2 * KY)


def accumulate(value, table, acc):
    acc[...] += lax.dot_general(
        table, value, (((1,), (1,)), ((), ())), preferred_element_type=jnp.float32
    )


def forward_kernel(scale, field_ref, coarse_ref, fine_ref, table_ref, et_ref, out_ref, acc):
    channels, rows_here, cols = field_ref.shape
    step = pl.program_id(0)

    @pl.when(step == 0)
    def _():
        acc[...] = jnp.zeros_like(acc)

    cos_fine, sin_fine = fine_ref[:KY], fine_ref[KY:]
    for group in range(cols // LANES):
        cos_coarse = coarse_ref[0, :KY, group : group + 1]
        sin_coarse = coarse_ref[0, KY:, group : group + 1]
        cosine = cos_coarse * cos_fine - sin_coarse * sin_fine
        sine = sin_coarse * cos_fine + cos_coarse * sin_fine
        et_ref[:, group * LANES : (group + 1) * LANES] = jnp.concatenate([cosine, -sine], axis=0).astype(jnp.bfloat16)
    accumulate(field_ref[...].reshape(channels * rows_here, cols), et_ref[...], acc)

    @pl.when(step == pl.num_programs(0) - 1)
    def _():
        transform_rows(channels, rows_here, scale, table_ref, acc, out_ref)


def prepare_hidden(y_ref, inverse_ref, hidden):
    channels = y_ref.shape[2]
    rows_here = inverse_ref.shape[0]
    depth = inverse_ref.shape[1] // 2
    lane = lax.broadcasted_iota(jnp.int32, (depth, LANES), 1)
    for o in range(channels):
        here = y_ref[:, :, o].reshape(depth, LANES)
        turned = jnp.where(lane < KY, -pltpu.roll(here, LANES - KY, 1), pltpu.roll(here, KY, 1))
        turned = jnp.where(lane < 2 * KY, turned, 0.0)
        part = jnp.dot(
            inverse_ref[...],
            jnp.concatenate([here, turned], axis=0),
            precision=lax.Precision.HIGHEST,
            preferred_element_type=jnp.float32,
        ).astype(jnp.bfloat16)
        for block in range(rows_here // XB):
            start = (block * channels + o) * XB
            hidden[start : start + XB, :] = part[block * XB : (block + 1) * XB, : 2 * KY]


def pointwise_matrix(layer, channels, weights_ref, kron):
    row = lax.broadcasted_iota(jnp.int32, (XB, channels * XB), 0)
    lane = lax.broadcasted_iota(jnp.int32, (XB, channels * XB), 1)
    for o in range(channels):
        value = jnp.zeros((XB, channels * XB), jnp.float32)
        for c in range(channels):
            value = jnp.where(lane == row + c * XB, weights_ref[layer * channels + o, c], value)
        kron[o * XB : (o + 1) * XB, :] = value.astype(jnp.bfloat16)


def spectral_values(et_ref, hidden, spectral):
    spectral[...] = jnp.dot(hidden[...], et_ref[...], preferred_element_type=jnp.float32)


def block_update(block, value_ref, kron, spectral):
    channels, _, cols = value_ref.shape
    size = channels * XB
    value = value_ref[:, block * XB : (block + 1) * XB, :].reshape(size, cols)
    local = jnp.dot(kron[...], value, preferred_element_type=jnp.float32)
    return jnp.tanh(local + spectral[block * size : (block + 1) * size, :] * (1.0 / KY))


def middle_kernel(
    layer, scale, value_ref, et_ref, y_ref, inverse_ref, weights_ref, table_ref, next_ref, out_ref, kron, hidden, spectral, acc
):
    channels, rows_here, cols = value_ref.shape
    step = pl.program_id(0)

    @pl.when(step == 0)
    def _():
        acc[...] = jnp.zeros_like(acc)
        prepare_hidden(y_ref, inverse_ref, hidden)
        pointwise_matrix(layer, channels, weights_ref, kron)

    spectral_values(et_ref, hidden, spectral)
    for block in range(rows_here // XB):
        updated = block_update(block, value_ref, kron, spectral).astype(jnp.bfloat16)
        next_ref[:, block * XB : (block + 1) * XB, :] = updated.reshape(channels, XB, cols)
    accumulate(next_ref[...].reshape(channels * rows_here, cols), et_ref[...], acc)

    @pl.when(step == pl.num_programs(0) - 1)
    def _():
        transform_rows(channels, rows_here, scale, table_ref, acc, out_ref)


def last_kernel(layer, value_ref, et_ref, y_ref, inverse_ref, weights_ref, image_ref, kron, hidden, spectral):
    channels, rows_here, cols = value_ref.shape

    @pl.when(pl.program_id(0) == 0)
    def _():
        prepare_hidden(y_ref, inverse_ref, hidden)
        pointwise_matrix(layer, channels, weights_ref, kron)

    spectral_values(et_ref, hidden, spectral)
    for block in range(rows_here // XB):
        updated = block_update(block, value_ref, kron, spectral).reshape(channels, XB, cols)
        total = weights_ref[LAYERS * channels, 0] * updated[0]
        for c in range(1, channels):
            total = total + weights_ref[LAYERS * channels, c] * updated[c]
        image_ref[block * XB : (block + 1) * XB, :] = total.astype(jnp.bfloat16)


def exchange_kernel(
    groups, per, spectrum_ref, same_ref, cross_ref, out_ref, partner_part, mine, arrived, mixed,
    pair_send, pair_recv, sum_send, sum_recv, mix_send, mix_recv, relay_send, relay_recv,
):
    clip = lax.axis_index("clip")
    row = lax.axis_index("trow")
    core = lax.axis_index("tcol")
    other = 1 - core
    channels = spectrum_ref.shape[2]

    if per < spectrum_ref.shape[3]:
        partner_part[...] = jnp.zeros_like(partner_part)
        arrived[...] = jnp.zeros_like(arrived)
        out_ref[...] = jnp.zeros_like(out_ref)

    barrier = pltpu.get_barrier_semaphore()
    pl.semaphore_signal(barrier, inc=1, device_id=(clip, row, other), device_id_type=MESH)
    for j in range(1, groups):
        peer = lax.rem(row + j, groups)
        pl.semaphore_signal(barrier, inc=1, device_id=(clip, peer, core), device_id_type=MESH)
    pl.semaphore_wait(barrier, groups)

    def used(ref):
        return ref.at[:, pl.ds(0, per), :]

    pairs = []
    for j in range(1, groups + 1):
        peer = lax.rem(row + j, groups)
        copy = pltpu.make_async_remote_copy(
            src_ref=used(spectrum_ref.at[other, peer]),
            dst_ref=used(partner_part.at[peer]),
            send_sem=pair_send.at[j - 1],
            recv_sem=pair_recv.at[j - 1],
            device_id=(clip, row, other),
            device_id_type=MESH,
        )
        copy.start()
        pairs.append(copy)
    sums = []
    for j in range(1, groups + 1):
        peer = lax.rem(row + j, groups)
        pairs[j - 1].wait_recv()
        mine[peer] = spectrum_ref[core, peer] + partner_part[peer]
        if j < groups:
            copy = pltpu.make_async_remote_copy(
                src_ref=used(mine.at[peer]),
                dst_ref=used(arrived.at[j - 1]),
                send_sem=sum_send.at[j - 1],
                recv_sem=sum_recv.at[j - 1],
                device_id=(clip, peer, core),
                device_id_type=MESH,
            )
            copy.start()
            sums.append(copy)
    total = mine[row]
    for j in range(1, groups):
        sums[j - 1].wait_recv()
        total = total + arrived[j - 1]

    lane = lax.broadcasted_iota(jnp.int32, total.shape[1:], 1)
    plain = [total[c] for c in range(channels)]
    swapped = [
        jnp.where(lane < KY, pltpu.roll(s, LANES - KY, 1), pltpu.roll(s, KY, 1)) for s in plain
    ]
    for o in range(channels):
        value = same_ref[o, 0] * plain[0] + cross_ref[o, 0] * swapped[0]
        for c in range(1, channels):
            value = value + (same_ref[o, c] * plain[c] + cross_ref[o, c] * swapped[c])
        mixed[o] = value
    out_ref[core, row] = mixed[...]

    sends = []
    for j in range(1, groups):
        peer = lax.rem(row + j, groups)
        copy = pltpu.make_async_remote_copy(
            src_ref=used(mixed),
            dst_ref=used(out_ref.at[core, row]),
            send_sem=mix_send.at[j - 1],
            recv_sem=mix_recv.at[j - 1],
            device_id=(clip, peer, core),
            device_id_type=MESH,
        )
        copy.start()
        sends.append(copy)
    relays = []
    for j in range(groups):
        source = lax.rem(row + groups - j, groups)
        if j:
            sends[j - 1].wait_recv()
        relay = pltpu.make_async_remote_copy(
            src_ref=used(mixed if j == 0 else out_ref.at[core, source]),
            dst_ref=used(out_ref.at[core, source]),
            send_sem=relay_send.at[j],
            recv_sem=relay_recv.at[j],
            device_id=(clip, row, other),
            device_id_type=MESH,
        )
        relay.start()
        relays.append(relay)
    for copy in pairs + sums + sends:
        copy.wait_send()
    for relay in relays:
        relay.wait()


def whole(shape):
    return pl.BlockSpec(shape, lambda i: (0,) * len(shape))


def exchange(spectrum, same, cross, groups, per, cid):
    chunk = spectrum.shape[2:]
    dma = pltpu.SemaphoreType.DMA
    vmem = pl.BlockSpec(memory_space=pltpu.VMEM)
    links = max(groups - 1, 1)
    return pl.pallas_call(
        functools.partial(exchange_kernel, groups, per),
        out_shape=jax.ShapeDtypeStruct(spectrum.shape, jnp.float32),
        in_specs=[vmem, vmem, vmem],
        out_specs=vmem,
        scratch_shapes=[
            pltpu.VMEM((groups,) + chunk, jnp.float32),
            pltpu.VMEM((groups,) + chunk, jnp.float32),
            pltpu.VMEM((links,) + chunk, jnp.float32),
            pltpu.VMEM(chunk, jnp.float32),
            dma((groups,)), dma((groups,)), dma((links,)), dma((links,)), dma((links,)), dma((links,)),
            dma((groups,)), dma((groups,)),
        ],
        compiler_params=pltpu.CompilerParams(
            collective_id=cid, has_side_effects=True, vmem_limit_bytes=VMEM_BYTES
        ),
        name=f"exchange_{cid}",
    )(spectrum, same, cross)


def body(groups, cores, field, pointwise, mixing, project):
    channels, rows_here, cols_here = field.shape
    total_rows = rows_here * groups
    total_cols = cols_here * cores
    row_index = lax.axis_index("trow")
    core_index = lax.axis_index("tcol")
    owners = groups * cores
    per = min(p for p in range(1, 2 * KY + 1) if 2 * KY % p == 0 and p * owners >= 2 * KY)
    sub = -(-per // SUB) * SUB
    scale = 1.0 / math.sqrt(total_rows * total_cols)
    tile = tile_of(cols_here)
    steps = cols_here // tile

    coarse, fine = column_seeds(core_index * cols_here, cols_here, tile, total_cols)
    cosine, sine = row_tables(row_index * rows_here, rows_here, total_rows, owners, per, sub)
    forward_table = jnp.concatenate([cosine, sine], axis=1)
    inverse_table = jnp.concatenate([cosine.T, sine.T], axis=1)

    first = (core_index * groups + row_index) * (per * KY)
    chunk = lax.dynamic_slice_in_dim(mixing, first, per * KY, 4)
    chunk = chunk.reshape(LAYERS, 2, channels, channels, per, KY).astype(jnp.float32)
    widths = ((0, 0), (0, 0), (0, 0), (0, sub - per), (0, LANES - 2 * KY))
    same = jnp.pad(jnp.concatenate([chunk[:, 0], chunk[:, 0]], axis=-1), widths)
    cross = jnp.pad(jnp.concatenate([-chunk[:, 1], chunk[:, 1]], axis=-1), widths)
    weights = jnp.concatenate([pointwise.reshape(LAYERS * channels, channels), project[None]], axis=0)
    weights = weights.astype(jnp.float32)

    spectrum_shape = (cores, groups, channels, sub, LANES)
    spectrum_type = jax.ShapeDtypeStruct(spectrum_shape, jnp.float32)
    value_spec = pl.BlockSpec((channels, rows_here, tile), lambda i: (0, 0, i))
    et_spec = pl.BlockSpec((2 * KY, tile), lambda i: (0, i))
    smem = pl.BlockSpec(memory_space=pltpu.SMEM)
    kron = pltpu.VMEM((channels * XB, channels * XB), jnp.bfloat16)
    hidden = pltpu.VMEM((channels * rows_here, 2 * KY), jnp.bfloat16)
    spectral = pltpu.VMEM((channels * rows_here, tile), jnp.float32)
    acc = pltpu.VMEM((2 * KY, channels * rows_here), jnp.float32)
    params = pltpu.CompilerParams(dimension_semantics=("arbitrary",), vmem_limit_bytes=VMEM_BYTES)

    columns, spectrum = pl.pallas_call(
        functools.partial(forward_kernel, scale),
        grid=(steps,),
        out_shape=(jax.ShapeDtypeStruct((2 * KY, cols_here), jnp.bfloat16), spectrum_type),
        in_specs=[
            value_spec,
            pl.BlockSpec((1,) + coarse.shape[1:], lambda i: (i, 0, 0)),
            whole(fine.shape),
            whole(forward_table.shape),
        ],
        out_specs=(et_spec, whole(spectrum_shape)),
        scratch_shapes=[acc],
        compiler_params=params,
        name="forward",
    )(field, coarse, fine, forward_table)

    current = field
    for layer in range(LAYERS):
        y = exchange(spectrum, same[layer], cross[layer], groups, per, layer)
        specs = [value_spec, et_spec, whole(spectrum_shape), whole(inverse_table.shape), smem]
        if layer + 1 < LAYERS:
            current, spectrum = pl.pallas_call(
                functools.partial(middle_kernel, layer, scale),
                grid=(steps,),
                out_shape=(jax.ShapeDtypeStruct(field.shape, jnp.bfloat16), spectrum_type),
                in_specs=specs + [whole(forward_table.shape)],
                out_specs=(value_spec, whole(spectrum_shape)),
                scratch_shapes=[kron, hidden, spectral, acc],
                compiler_params=params,
                name="middle",
            )(current, columns, y, inverse_table, weights, forward_table)
        else:
            image = pl.pallas_call(
                functools.partial(last_kernel, layer),
                grid=(steps,),
                out_shape=jax.ShapeDtypeStruct((rows_here, cols_here), jnp.bfloat16),
                in_specs=specs,
                out_specs=pl.BlockSpec((rows_here, tile), lambda i: (0, i)),
                scratch_shapes=[kron, hidden, spectral],
                compiler_params=params,
                name="last",
            )(current, columns, y, inverse_table, weights)
    return image


def solution(mesh):
    groups, cores = mesh.shape["trow"], mesh.shape["tcol"]
    in_specs = (P(None, ("clip", "trow"), "tcol"), P(), P(), P())
    out_specs = P(("clip", "trow"), "tcol")
    return jax.shard_map(
        functools.partial(body, groups, cores), mesh=mesh, in_specs=in_specs, out_specs=out_specs, check_vma=False
    )
```

time: 107 us -> 86.9 us (0.81)
  other arithmetic: 15.9 us -> 5.14 us
  Pallas kernels: 84.4 us -> 77.9 us
  local copies, waits for them, and re-layouts: 5.71 us -> 3.02 us
    unnamed x4 -> x0, other arithmetic: 11.7 us -> none
    pallas_call x4, Pallas kernels: 74.7 us -> 68.1 us  [the longest x2 41.2 us: exchange(): pl.pallas_call(functools.partial(exchange_kernel, groups, per), out_shape...]
    mul x3 -> x0, local copies, waits for them, and re-layouts: 2.27 us -> none  [body(): krons = [jnp.kron(pointwise[layer], eye) for layer in range(LAYERS)]]
    unnamed x3 -> x0, local copies, waits for them, and re-layouts: 1.37 us -> none
where the time goes in v1:
time: 86.9 us; the launch traced here: 86.1 us
  Pallas kernels  77.9 us (90%)
  other arithmetic  5.14 us (6%)
  local copies, waits for them, and re-layouts  3.02 us (3%)
    pallas_call x2, Pallas kernels, exchange(): pl.pallas_call(functools.partial(exchange_kernel, groups, per), out_shape...  41.2 us
    pallas_call x1, Pallas kernels, body(): pl.pallas_call(functools.partial(middle_kernel, layer, scale), grid=(step...  15.5 us
    pallas_call x1, Pallas kernels, body(): pl.pallas_call(functools.partial(last_kernel, layer), grid=(steps,), out_...  11.3 us
    pallas_call x1, Pallas kernels, body(): pl.pallas_call(functools.partial(forward_kernel, scale), grid=(steps,), o...  9.8 us

profile of v1, /device:TPU:0, one launch (start us, length us, event | category | flops | bytes accessed | tf_op | source)
XLA Modules:
  0.0 86.1 jit_solution(8780712298725009141)
XLA Ops:
  0.0 1.3 %maximum_convert_fusion.weights_ref = f32[17,8]{1,0:T(8,128)} fusion(bf16[1,8]{1,0:T(2,128)(2,1)} %bitcast.23, bf16[16,8]{1,0:T(8,128)(2,1)} %bitcast.22), kind=kLoop, calls=%fused_computation.57 | loop fusion | flops 544 | bytes 816 | tf_op jit(solution)/shard_map/convert_element_type | solution.py:343
  1.4 0.1 fusion.21
  1.5 0.1 pad_maximum_fusion.3
  1.6 0.1 fusion.18
  1.7 0.6 pad_maximum_fusion.2.fine_ref
  2.3 0.6 cosine_select_fusion
  2.9 0.7 pad_maximum_fusion
  3.7 0.9 %copy.18.coarse_ref = f32[8,96,4]{2,1,0:T(8,128)} copy(f32[8,96,4]{1,0,2:T(8,128)S(1)} %pad_maximum_fusion.3) | data formatting | bytes 24576 | tf_op jit(solution)/shard_map/concatenate | solution.py:38
  4.6 1.1 %dynamic-slice_convert_fusion = f32[2,2,8,8,288]{4,3,2,1,0:T(8,128)S(1)} fusion(bf16[2,2,8,8,4608]{4,3,2,1,0:T(8,128)(2,1)} %param.6, s32[]{:T(128)S(6)} %select_n.116), kind=kLoop, calls=%fused_computation.10 | loop fusion | flops 73728 | bytes 442372 | tf_op jit(solution)/shard_map/convert_element_type | solution.py:338
  5.7 0.3 reshape.60
  6.0 0.1 fusion.25
  6.1 0.1 slice_bitcast_fusion
  6.2 0.4 select_maximum_fusion
  6.5 0.8 slice_bitcast_fusion.2
  7.4 0.8 slice_bitcast_fusion.3
  8.2 9.8 %forward.1 = (bf16[96,4096]{1,0:T(8,128)(2,1)}, f32[2,8,8,8,128]{4,3,2,1,0:T(8,128)}) custom-call(bf16[8,128,4096]{2,1,0:T(8,128)(2,1)} %value_ref.1, f32[8,96,4]{2,1,0:T(8,128)} %copy.18.coarse_ref, f32[96,128]{1,0:T(8,128)} %pad_maximum_fusion.2.fine_ref, f32[128,256]{1,0:T(8,128)} %get-tuple-element.27.table_ref), custom_call_target="tpu_custom_call" | custom-call | tf_op jit(solution)/shard_map/forward/pallas_call | solution.py:356
  18.0 21.4 %exchange_0.1.y_ref = f32[2,8,8,8,128]{4,3,2,1,0:T(8,128)} custom-call(f32[2,8,8,8,128]{4,3,2,1,0:T(8,128)} %get-tuple-element.10.spectrum_ref, f32[8,8,8,128]{3,2,1,0:T(8,128)} %get-tuple-element.18.same_ref, f32[8,8,8,128]{3,2,1,0:T(8,128)} %get-tuple-element.16.cross_ref), custom_call_target="tpu_custom_call" | custom-call | tf_op jit(solution)/shard_map/exchange_0/pallas_call | solution.py:298
  39.5 15.5 %middle.1 = (bf16[8,128,4096]{2,1,0:T(8,128)(2,1)}, f32[2,8,8,8,128]{4,3,2,1,0:T(8,128)}) custom-call(bf16[8,128,4096]{2,1,0:T(8,128)(2,1)} %value_ref.1, bf16[96,4096]{1,0:T(8,128)(2,1)} %get-tuple-element.9.et_ref, f32[2,8,8,8,128]{4,3,2,1,0:T(8,128)} %exchange_0.1.y_ref, f32[128,256]{1,0:T(8,128)} %get-tuple-element.28.inverse_ref, ...), custom_call_target="tpu_custom_call" | custom-call | tf_op jit(solution)/shard_map/middle/pallas_call | solution.py:377
  55.0 19.8 %exchange_1.1.y_ref = f32[2,8,8,8,128]{4,3,2,1,0:T(8,128)} custom-call(f32[2,8,8,8,128]{4,3,2,1,0:T(8,128)} %get-tuple-element.12.spectrum_ref, f32[8,8,8,128]{3,2,1,0:T(8,128)} %get-tuple-element.17.same_ref, f32[8,8,8,128]{3,2,1,0:T(8,128)} %get-tuple-element.15.cross_ref), custom_call_target="tpu_custom_call" | custom-call | tf_op jit(solution)/shard_map/exchange_1/pallas_call | solution.py:298
  74.8 11.3 %last.1 = bf16[128,4096]{1,0:T(8,128)(2,1)} custom-call(bf16[8,128,4096]{2,1,0:T(8,128)(2,1)} %get-tuple-element.11.value_ref, bf16[96,4096]{1,0:T(8,128)(2,1)} %get-tuple-element.9.et_ref, f32[2,8,8,8,128]{4,3,2,1,0:T(8,128)} %exchange_1.1.y_ref, f32[128,256]{1,0:T(8,128)} %get-tuple-element.28.inverse_ref, f32[17,8]{1,0:T(8,128)} %maximum_convert_fusion.weights_ref), custom_call_target="tpu_custom_call" | custom-call | tf_op jit(solution)/shard_map/last/pallas_call | solution.py:388
  (4 shorter events, 0.0 us)

commit v2 on v1

--- a/solution.py
+++ b/solution.py
@@ -182,7 +182,7 @@
 
 
 def exchange_kernel(
-    groups, per, spectrum_ref, same_ref, cross_ref, out_ref, partner_part, mine, arrived, mixed,
+    groups, per, layer, spectrum_ref, same_ref, cross_ref, out_ref, partner_part, mine, arrived, mixed,
     pair_send, pair_recv, sum_send, sum_recv, mix_send, mix_recv, relay_send, relay_recv,
 ):
     clip = lax.axis_index("clip")
@@ -246,9 +246,9 @@
         jnp.where(lane < KY, pltpu.roll(s, LANES - KY, 1), pltpu.roll(s, KY, 1)) for s in plain
     ]
     for o in range(channels):
-        value = same_ref[o, 0] * plain[0] + cross_ref[o, 0] * swapped[0]
+        value = same_ref[layer, o, 0] * plain[0] + cross_ref[layer, o, 0] * swapped[0]
         for c in range(1, channels):
-            value = value + (same_ref[o, c] * plain[c] + cross_ref[o, c] * swapped[c])
+            value = value + (same_ref[layer, o, c] * plain[c] + cross_ref[layer, o, c] * swapped[c])
         mixed[o] = value
     out_ref[core, row] = mixed[...]
 
@@ -296,7 +296,7 @@
     vmem = pl.BlockSpec(memory_space=pltpu.VMEM)
     links = max(groups - 1, 1)
     return pl.pallas_call(
-        functools.partial(exchange_kernel, groups, per),
+        functools.partial(exchange_kernel, groups, per, cid),
         out_shape=jax.ShapeDtypeStruct(spectrum.shape, jnp.float32),
         in_specs=[vmem, vmem, vmem],
         out_specs=vmem,
@@ -371,7 +371,7 @@
 
     current = field
     for layer in range(LAYERS):
-        y = exchange(spectrum, same[layer], cross[layer], groups, per, layer)
+        y = exchange(spectrum, same, cross, groups, per, layer)
         specs = [value_spec, et_spec, whole(spectrum_shape), whole(inverse_table.shape), smem]
         if layer + 1 < LAYERS:
             current, spectrum = pl.pallas_call(

time: 86.9 us -> 86.6 us (level)
  local copies, waits for them, and re-layouts: 3.02 us -> 1.35 us
  other arithmetic: 5.14 us -> 6.14 us
    squeeze x2 -> x0, local copies, waits for them, and re-layouts: 1.68 us -> none  [body(): y = exchange(spectrum, same[layer], cross[layer], groups, per, layer)]
    concatenate x1, other arithmetic: 0.37 us -> 1.38 us  [body(): jnp.concatenate([-chunk[:, 1], chunk[:, 1]], axis=-1)]
where the time goes in v2:
time: 86.6 us; the launch traced here: 85.8 us
  Pallas kernels  78.2 us (90%)
  other arithmetic  6.14 us (7%)
  local copies, waits for them, and re-layouts  1.35 us (2%)
    pallas_call x2, Pallas kernels, exchange(): pl.pallas_call(functools.partial(exchange_kernel, groups, per, cid), out_...  41.6 us
    pallas_call x1, Pallas kernels, body(): pl.pallas_call(functools.partial(middle_kernel, layer, scale), grid=(step...  15.5 us
    pallas_call x1, Pallas kernels, body(): pl.pallas_call(functools.partial(last_kernel, layer), grid=(steps,), out_...  11.3 us
    pallas_call x1, Pallas kernels, body(): pl.pallas_call(functools.partial(forward_kernel, scale), grid=(steps,), o...  9.77 us

profile of v2, /device:TPU:0, one launch (start us, length us, event | category | flops | bytes accessed | tf_op | source)
XLA Modules:
  0.0 85.8 jit_solution(15134524676701843671)
XLA Ops:
  0.0 1.3 %maximum_convert_fusion.weights_ref = f32[17,8]{1,0:T(8,128)} fusion(bf16[1,8]{1,0:T(2,128)(2,1)} %bitcast.15, bf16[16,8]{1,0:T(8,128)(2,1)} %bitcast.14), kind=kLoop, calls=%fused_computation.53 | loop fusion | flops 544 | bytes 816 | tf_op jit(solution)/shard_map/convert_element_type | solution.py:343
  1.3 0.1 fusion.21
  1.5 0.1 pad_maximum_fusion.3
  1.6 0.1 fusion.18
  1.7 0.6 pad_maximum_fusion.2.fine_ref
  2.3 0.6 cosine_select_fusion
  2.9 0.7 pad_maximum_fusion
  3.7 0.9 %copy.18.coarse_ref = f32[8,96,4]{2,1,0:T(8,128)} copy(f32[8,96,4]{1,0,2:T(8,128)S(1)} %pad_maximum_fusion.3) | data formatting | bytes 24576 | tf_op jit(solution)/shard_map/concatenate | solution.py:38
  4.6 1.1 %dynamic-slice_convert_fusion = f32[2,2,8,8,288]{4,3,2,1,0:T(8,128)S(1)} fusion(bf16[2,2,8,8,4608]{4,3,2,1,0:T(8,128)(2,1)} %param.6, s32[]{:T(128)S(6)} %select_n.116), kind=kLoop, calls=%fused_computation.6 | loop fusion | flops 73728 | bytes 442372 | tf_op jit(solution)/shard_map/convert_element_type | solution.py:338
  5.7 0.3 reshape.60
  6.0 0.1 fusion.25
  6.1 0.1 slice_bitcast_fusion
  6.2 1.4 %select_maximum_fusion = (f32[2,8,8,8,128]{4,3,2,1,0:T(8,128)}, f32[2,8,8,8,128]{4,3,2,1,0:T(8,128)}) fusion(f32[2,8,8,6,48]{4,3,2,1,0:T(8,128)S(1)} %get-tuple-element.13, f32[2,8,8,6,48]{4,3,2,1,0:T(8,128)S(1)} %fusion.25, f32[2,8,8,6,48]{4,3,2,1,0:T(8,128)S(1)} %get-tuple-element.14), kind=kLoop, calls=%fused_computation | loop fusion | flops 1703936 | bytes 1490944 | tf_op jit(solution)/shard_map/concatenate | solution.py:341
  7.5 9.8 %forward.1 = (bf16[96,4096]{1,0:T(8,128)(2,1)}, f32[2,8,8,8,128]{4,3,2,1,0:T(8,128)}) custom-call(bf16[8,128,4096]{2,1,0:T(8,128)(2,1)} %value_ref.1, f32[8,96,4]{2,1,0:T(8,128)} %copy.18.coarse_ref, f32[96,128]{1,0:T(8,128)} %pad_maximum_fusion.2.fine_ref, f32[128,256]{1,0:T(8,128)} %get-tuple-element.23.table_ref), custom_call_target="tpu_custom_call" | custom-call | tf_op jit(solution)/shard_map/forward/pallas_call | solution.py:356
  17.3 21.6 %exchange_0.1.y_ref = f32[2,8,8,8,128]{4,3,2,1,0:T(8,128)} custom-call(f32[2,8,8,8,128]{4,3,2,1,0:T(8,128)} %get-tuple-element.10.spectrum_ref, f32[2,8,8,8,128]{4,3,2,1,0:T(8,128)} %get-tuple-element.26.same_ref, f32[2,8,8,8,128]{4,3,2,1,0:T(8,128)} %get-tuple-element.25.cross_ref), custom_call_target="tpu_custom_call" | custom-call | tf_op jit(solution)/shard_map/exchange_0/pallas_call | solution.py:298
  39.0 15.5 %middle.1 = (bf16[8,128,4096]{2,1,0:T(8,128)(2,1)}, f32[2,8,8,8,128]{4,3,2,1,0:T(8,128)}) custom-call(bf16[8,128,4096]{2,1,0:T(8,128)(2,1)} %value_ref.1, bf16[96,4096]{1,0:T(8,128)(2,1)} %get-tuple-element.9.et_ref, f32[2,8,8,8,128]{4,3,2,1,0:T(8,128)} %exchange_0.1.y_ref, f32[128,256]{1,0:T(8,128)} %get-tuple-element.24.inverse_ref, ...), custom_call_target="tpu_custom_call" | custom-call | tf_op jit(solution)/shard_map/middle/pallas_call | solution.py:377
  54.5 20.0 %exchange_1.1.y_ref = f32[2,8,8,8,128]{4,3,2,1,0:T(8,128)} custom-call(f32[2,8,8,8,128]{4,3,2,1,0:T(8,128)} %get-tuple-element.12.spectrum_ref, f32[2,8,8,8,128]{4,3,2,1,0:T(8,128)} %get-tuple-element.26.same_ref, f32[2,8,8,8,128]{4,3,2,1,0:T(8,128)} %get-tuple-element.25.cross_ref), custom_call_target="tpu_custom_call" | custom-call | tf_op jit(solution)/shard_map/exchange_1/pallas_call | solution.py:298
  74.5 11.3 %last.1 = bf16[128,4096]{1,0:T(8,128)(2,1)} custom-call(bf16[8,128,4096]{2,1,0:T(8,128)(2,1)} %get-tuple-element.11.value_ref, bf16[96,4096]{1,0:T(8,128)(2,1)} %get-tuple-element.9.et_ref, f32[2,8,8,8,128]{4,3,2,1,0:T(8,128)} %exchange_1.1.y_ref, f32[128,256]{1,0:T(8,128)} %get-tuple-element.24.inverse_ref, f32[17,8]{1,0:T(8,128)} %maximum_convert_fusion.weights_ref), custom_call_target="tpu_custom_call" | custom-call | tf_op jit(solution)/shard_map/last/pallas_call | solution.py:388
  (4 shorter events, 0.0 us)
